TPU v7x, 512 devices: a whole 4x8x8 slice. The times are simulated.
512 devices in a mesh: row: 8 (over z_lo, x), col: 8 (over z_hi, core), panel: 8 (over y).
Axes of the slice: x: 4, y: 8, z: 8 (z_hi: 4, z_lo: 2; z = z_hi * 2 + z_lo), core: 2. Of those that a mesh axis runs over, the one named last changes fastest.
Arguments:
- velocity: bfloat16 [4608, 6, 4096], P(('row', 'col'), None, 'panel'), may hold values from -6 to 6
- panel_weight: float32 [4096], P('panel'), may hold values from -0.109375 to 0.109375
- panel_group: int32 [4096], P('panel'), may hold values from 0 to 3
- tile_map: int32 [8, 8], replicated, may hold values from 0 to 3
- group_gain: float32 [4, 4], replicated, may hold values from 0.25 to 1
Outputs:
- qtf: float32 [4608, 2, 4608], P(('row', 'panel'), None, 'col')
All inputs are finite; a program needn't handle non-finite values.
Results may differ from a plain program's by a relative error of at most 0.0029.
Values may be sent and summed in bfloat16 or wider, within the bound.
A program may use at most 64 MiB of HBM per device.

v0:
```python
import jax
import jax.numpy as jnp
from jax import lax
from jax.sharding import PartitionSpec as P


def spread(value, axis, source):
    kept = jnp.where(lax.axis_index(axis) == source, value, 0).astype(value.dtype)
    return lax.psum(kept, axis)


def contract(left_side, right_side):
    return lax.dot_general(
        left_side, right_side, (((1,), (1,)), ((), ())), preferred_element_type=jnp.float32
    )


def pair_products(row_piece, right_side, tile_sign, half_depth):
    left_re = row_piece[:, :half_depth]
    left_im = row_piece[:, half_depth:]
    right_re = right_side[:, :half_depth]
    right_im = right_side[:, half_depth:]
    real_part = contract(left_re, right_re) + tile_sign * contract(left_im, right_im)
    imag_part = contract(left_im, right_re) - tile_sign * contract(left_re, right_im)
    return jnp.stack((real_part, imag_part), axis=1)


def local(velocity, panel_weight, panel_group, tile_map, group_gain):
    row_index = lax.axis_index("row")
    col_index = lax.axis_index("col")
    rows_block = lax.all_gather(velocity, "col", axis=0, tiled=True)
    cols_block = spread(rows_block, "row", col_index)
    chosen = (lax.broadcasted_iota(jnp.int32, tile_map.shape, 0) == row_index) & (
        lax.broadcasted_iota(jnp.int32, tile_map.shape, 1) == col_index
    )
    region = jnp.sum(jnp.where(chosen, tile_map, 0))
    group_count = group_gain.shape[0]
    case_cols = lax.broadcasted_iota(jnp.int32, group_gain.shape, 1)
    case_gains = jnp.sum(jnp.where(case_cols == region, group_gain, jnp.float32(0.0)), axis=1)
    group_ids = lax.broadcasted_iota(jnp.int32, (panel_group.shape[0], group_count), 1)
    panel_gain = jnp.sum(
        jnp.where(panel_group[:, None] == group_ids, case_gains[None, :], jnp.float32(0.0)), axis=1
    )
    panel_scale = panel_weight * panel_gain
    weighted = (rows_block.astype(jnp.float32) * panel_scale[None, None, :]).astype(jnp.bfloat16)
    tile_width = weighted.shape[0]
    slab_size = weighted.shape[2]
    left_side = weighted.reshape(tile_width, 6 * slab_size)
    right_side = cols_block.reshape(cols_block.shape[0], 6 * slab_size)
    tile_sign = jnp.where(row_index <= col_index, jnp.float32(1.0), jnp.float32(-1.0))
    half_depth = 3 * slab_size
    partial_tile = pair_products(left_side, right_side, tile_sign, half_depth)
    result = lax.psum_scatter(partial_tile, "panel", scatter_dimension=0, tiled=True)
    return result


def solution(mesh):
    return jax.shard_map(
        local,
        mesh=mesh,
        in_specs=(P(("row", "col"), None, "panel"), P("panel"), P("panel"), P(), P()),
        out_specs=P(("row", "panel"), None, "col"),
        check_vma=False,
    )
```

profile of v0, /device:TPU:4, one launch (start us, length us, event | category | flops | bytes accessed | tf_op | source)
XLA Modules:
  0.0 246.8 jit_solution(13272052365680096868)
XLA Ops:
  6.5 0.0 all-gather.2.cloned.1.call-start
  6.5 0.7 all-gather.2.cloned.1.call-update
  7.3 0.0 all-reduce.2.cloned.1.call-start
  7.3 57.7 %all-gather.2.cloned.1.call-done = bf16[576,6,512]{2,0,1:T(8,128)(2,1)} async-done(((bf16[72,6,512]{2,0,1:T(8,128)(2,1)}), bf16[576,6,512]{2,0,1:T(8,128)(2,1)}) %all-gather.2.cloned.1.call-update) | async-done | bytes 3538960 | tf_op jit(solution)/shard_map/all_gather | solution.py:31
  65.0 0.2 broadcast_select_fusion
  65.2 3.9 %copy.11 = bf16[576,6,512]{0,2,1:T(8,128)(2,1)} copy(bf16[576,6,512]{2,0,1:T(8,128)(2,1)S(1)} %broadcast_select_fusion) | data formatting | bytes 7077888 | tf_op jit(solution)/shard_map/jit(_where)/select_n | solution.py:8
  69.1 0.0 copy-start.2
  69.1 0.0 copy-start
  69.2 0.0 all-reduce.2.cloned.1.call-update
  69.2 0.0 reduce-scatter.2.cloned.1.call-start
  69.2 0.6 copy-done.2
  69.8 0.7 select_reduce_fusion.1
  70.5 0.6 iota_compare_fusion.3
  71.2 0.0 copy-done.4
  71.2 0.1 select_reduce_fusion.2
  71.3 0.0 copy-done.5
  71.3 0.1 select_reduce_fusion
  71.4 0.0 copy-done.3
  71.4 0.0 copy-done
  71.4 2.6 %multiply_convert_fusion = bf16[576,6,512]{2,0,1:T(8,128)(2,1)} fusion(bf16[576,6,512]{2,0,1:T(8,128)(2,1)S(1)} %copy-done, f32[512]{0:T(512)S(1)} %mul.21), kind=kLoop, calls=%fused_computation | loop fusion | flops 5308416 | bytes 7079936 | tf_op jit(solution)/shard_map/convert_element_type | solution.py:45
  74.0 5.9 %copy.10 = bf16[576,6,512]{0,2,1:T(8,128)(2,1)} copy(bf16[576,6,512]{2,0,1:T(8,128)(2,1)} %multiply_convert_fusion) | data formatting | bytes 7077888 | tf_op jit(solution)/shard_map/convert_element_type | solution.py:45
  79.9 97.6 %all-reduce.2.cloned.1.call-done = bf16[576,3072]{0,1:T(8,128)(2,1)} async-done(((bf16[576,3072]{0,1:T(8,128)(2,1)}), bf16[576,3072]{0,1:T(8,128)(2,1)}) %all-reduce.2.cloned.1.call-update) | async-done | bytes 3538960 | tf_op jit(solution)/shard_map/psum | solution.py:9
  177.5 3.9 %fusion = f32[576,576]{1,0:T(8,128)S(1)} fusion(bf16[576,3072]{0,1:T(8,128)(2,1)} %all-reduce.2.cloned.1.call-done, bf16[576,3072]{0,1:T(8,128)(2,1)} %bitcast.7), kind=kOutput, calls=%fused_computation.3 | convolution fusion | flops 1019215872 | bytes 5259264 | tf_op jit(solution)/shard_map/dot_general | solution.py:13
  181.4 0.0 copy-done.1
  181.4 0.6 copy-done.6
  182.0 1.6 fusion.2
  183.6 1.6 subtract_bitcast_fusion
  185.2 1.6 add_bitcast_fusion
  186.8 1.8 pad_maximum_fusion
  188.6 0.0 reduce-scatter.2.cloned.1.call-update
  188.6 49.7 %reduce-scatter.2.cloned.1.call-done = f32[72,2,576]{2,0,1:T(8,128)} async-done(((f32[576,2,576]{2,0,1:T(8,128)}), f32[72,2,576]{2,0,1:T(8,128)}) %reduce-scatter.2.cloned.1.call-update) | async-done | bytes 331792 | tf_op jit(solution)/shard_map/reduce_scatter | solution.py:53
  238.4 1.9 copy.12
  (7 shorter events, 0.0 us)
Async XLA Ops:
  6.5 58.5 %all-gather.2.cloned.1.call-start = ((), (), s32[]{:S(2)}) async-start(), calls=%async_computation.1 | async-start | bytes 3981312 | tf_op jit(solution)/shard_map/all_gather | solution.py:31
  7.3 170.3 %all-reduce.2.cloned.1.call-start = ((), (), s32[]{:S(2)}) async-start(), calls=%async_computation.2 | async-start | bytes 7864320 | tf_op jit(solution)/shard_map/psum | solution.py:9
  69.1 0.7 copy-start.2
  69.1 2.0 copy-start.4
  69.1 2.2 copy-start.5
  69.1 2.3 copy-start.3
  69.1 2.3 copy-start
  69.2 169.2 %reduce-scatter.2.cloned.1.call-start = ((), (), s32[]{:S(2)}) async-start(), calls=%async_computation.3 | async-start | bytes 3317760 | tf_op jit(solution)/shard_map/reduce_scatter | solution.py:53
  177.5 3.9 %copy-start.1 = (bf16[576,6,512]{0,2,1:T(8,128)(2,1)S(1)}, bf16[576,6,512]{0,2,1:T(8,128)(2,1)}, u32[]{:S(2)}) copy-start(bf16[576,6,512]{0,2,1:T(8,128)(2,1)} %copy.10) | copy-start | bytes 10616836
  177.5 4.5 %copy-start.6 = (bf16[576,3072]{0,1:T(8,128)(2,1)S(1)}, bf16[576,3072]{0,1:T(8,128)(2,1)}, u32[]{:S(2)}) copy-start(bf16[576,3072]{0,1:T(8,128)(2,1)} %all-reduce.2.cloned.1.call-done) | copy-start | bytes 10616836
Sparse Core Ops, SparseCore 0:
  9.5 55.4 all-gather.1
  69.3 108.1 all-reduce.1
  188.7 49.5 reduce-scatter.1
where the time goes:
time: 247 us
  waiting for transfers between devices  206 us (83%)
  between operations  13.2 us (5%)
  local copies, waits for them, and re-layouts  12.9 us (5%)
  matrix products  8.64 us (3%)
  other arithmetic  6.18 us (3%)
    psum x1, waiting for transfers between devices, spread(): return lax.psum(kept, axis)  97.6 us
    all_gather x1, waiting for transfers between devices, local(): rows_block = lax.all_gather(velocity, 'col', axis=0, tiled=True)  57.7 us
    reduce_scatter x1, waiting for transfers between devices, local(): lax.psum_scatter(partial_tile, 'panel', scatter_dimension=0, tiled=True)  49.7 us
    dot_general x4, matrix products, contract(): lax.dot_general(left_side, right_side, (((1,), (1,)), ((), ())), preferre...  8.64 us
    convert_element_type x1, local copies, waits for them, and re-layouts, local(): (rows_block.astype(jnp.float32) * panel_scale[None, None, :]).astype(jnp....  5.93 us
  transfers between devices with their start and end apart: 3, of which 3 were waited for; matrix products, arithmetic and copies ran while one was open for 4% of the time, Pallas kernels for 0%

commit v1 on v0

--- a/solution.py
+++ b/solution.py
@@ -2,11 +2,17 @@
 import jax.numpy as jnp
 from jax import lax
 from jax.sharding import PartitionSpec as P
+from jax.lax import all_gather
 
 
 def spread(value, axis, source):
     kept = jnp.where(lax.axis_index(axis) == source, value, 0).astype(value.dtype)
-    return lax.psum(kept, axis)
+
+    def targets_assign(message):
+        response = all_gather(message, axis).sum(axis=0)
+        return response
+
+    return targets_assign(kept)
 
 
 def contract(left_side, right_side):

time: 247 us -> 436 us (1.77)
  waiting for transfers between devices: 206 us -> 378 us
  other arithmetic: 6.18 us -> 22.4 us
    all_gather x0 -> x1, waiting for transfers between devices: none -> 270 us  [targets_assign(): response = all_gather(message, axis).sum(axis=0)]
    psum x1 -> x0, waiting for transfers between devices: 97.6 us -> none  [spread(): return lax.psum(kept, axis)]
    reduce_sum x0 -> x1, other arithmetic: none -> 14.5 us  [targets_assign(): response = all_gather(message, axis).sum(axis=0)]
  transfers between devices with their start and end apart: 3 -> 3, of which waited for: 3 -> 3; matrix products, arithmetic and copies ran while one was open for 4% -> 2% of each run, Pallas kernels for 0% -> 0%
where the time goes in v1:
time: 436 us
  waiting for transfers between devices  378 us (87%)
  other arithmetic  22.4 us (5%)
  between operations  13.2 us (3%)
  local copies, waits for them, and re-layouts  13 us (3%)
  matrix products  8.64 us (2%)
    all_gather x1, waiting for transfers between devices, targets_assign(): response = all_gather(message, axis).sum(axis=0)  270 us
    all_gather x1, waiting for transfers between devices, local(): rows_block = lax.all_gather(velocity, 'col', axis=0, tiled=True)  57.7 us
    reduce_scatter x1, waiting for transfers between devices, local(): lax.psum_scatter(partial_tile, 'panel', scatter_dimension=0, tiled=True)  49.6 us
    reduce_sum x1, other arithmetic, targets_assign(): response = all_gather(message, axis).sum(axis=0)  14.5 us
  transfers between devices with their start and end apart: 3, of which 3 were waited for; matrix products, arithmetic and copies ran while one was open for 2% of the time, Pallas kernels for 0%

profile of v1, /device:TPU:4, one launch (start us, length us, event | category | flops | bytes accessed | tf_op | source)
XLA Modules:
  0.0 435.8 jit_solution(751372124546751644)
XLA Ops:
  6.5 0.0 all-gather.4.cloned.1.call-start
  6.5 0.7 all-gather.4.cloned.1.call-update
  7.3 0.0 all-gather.6.cloned.1.call-start
  7.3 57.7 %all-gather.4.cloned.1.call-done = bf16[576,6,512]{2,0,1:T(8,128)(2,1)} async-done(((bf16[72,6,512]{2,0,1:T(8,128)(2,1)}), bf16[576,6,512]{2,0,1:T(8,128)(2,1)}) %all-gather.4.cloned.1.call-update) | async-done | bytes 3538960 | tf_op jit(solution)/shard_map/all_gather | solution.py:37
  65.0 2.0 broadcast_select_fusion
  67.0 0.0 copy-start
  67.0 0.0 all-gather.6.cloned.1.call-update
  67.1 0.0 reduce-scatter.2.cloned.1.call-start
  67.1 0.6 copy-done.3
  67.7 0.7 select_reduce_fusion.1
  68.4 0.6 iota_compare_fusion.3
  69.1 0.0 copy-done.5
  69.1 0.1 select_reduce_fusion.2
  69.2 0.0 copy-done.6
  69.2 0.1 select_reduce_fusion
  69.3 0.0 copy-done.4
  69.3 0.0 copy-done
  69.3 2.5 multiply_convert_fusion
  71.8 5.9 %copy.12 = bf16[576,6,512]{0,2,1:T(8,128)(2,1)} copy(bf16[576,6,512]{2,0,1:T(8,128)(2,1)} %multiply_convert_fusion) | data formatting | bytes 7077888 | tf_op jit(solution)/shard_map/convert_element_type | solution.py:51
  77.8 270.4 %all-gather.6.cloned.1.call-done = bf16[4608,6,512]{2,0,1:T(8,128)(2,1)} async-done(((bf16[576,6,512]{2,0,1:T(8,128)(2,1)}), bf16[4608,6,512]{2,0,1:T(8,128)(2,1)}) %all-gather.6.cloned.1.call-update) | async-done | bytes 28311568 | tf_op jit(solution)/shard_map/all_gather | solution.py:12
  348.2 14.5 %reduce_sum.42 = bf16[576,6,512]{2,0,1:T(8,128)(2,1)S(1)} reduce(bf16[8,576,6,512]{3,1,0,2:T(8,128)(2,1)} %bitcast.7, bf16[]{:T(256)} %constant.17.clone.1), dimensions={0}, to_apply=%region_3.4 | reduce | flops 12386304 | bytes 31850498 | tf_op jit(solution)/shard_map/reduce_sum | solution.py:12
  362.7 3.9 copy.13
  366.6 3.9 fusion
  370.5 0.0 copy-done.1
  370.5 0.6 copy-done.2
  371.1 1.6 fusion.2
  372.7 1.6 subtract_bitcast_fusion
  374.3 1.6 add_bitcast_fusion
  375.9 1.8 pad_maximum_fusion
  377.7 0.0 reduce-scatter.2.cloned.1.call-update
  377.7 49.6 %reduce-scatter.2.cloned.1.call-done = f32[72,2,576]{2,0,1:T(8,128)} async-done(((f32[576,2,576]{2,0,1:T(8,128)}), f32[72,2,576]{2,0,1:T(8,128)}) %reduce-scatter.2.cloned.1.call-update) | async-done | bytes 331792 | tf_op jit(solution)/shard_map/reduce_scatter | solution.py:59
  427.3 1.9 copy.14
  (8 shorter events, 0.0 us)
Async XLA Ops:
  6.5 58.5 %all-gather.4.cloned.1.call-start = ((), (), s32[]{:S(2)}) async-start(), calls=%async_computation.1 | async-start | bytes 3981312 | tf_op jit(solution)/shard_map/all_gather | solution.py:37
  7.3 340.9 %all-gather.6.cloned.1.call-start = ((), (), s32[]{:S(2)}) async-start(), calls=%async_computation.3 | async-start | bytes 31850496 | tf_op jit(solution)/shard_map/all_gather | solution.py:12
  67.0 0.7 copy-start.3
  67.0 2.0 copy-start.5
  67.0 2.2 copy-start.6
  67.0 2.3 copy-start.4
  67.0 2.3 copy-start
  67.1 360.3 %reduce-scatter.2.cloned.1.call-start = ((), (), s32[]{:S(2)}) async-start(), calls=%async_computation.2 | async-start | bytes 3317760 | tf_op jit(solution)/shard_map/reduce_scatter | solution.py:59
  366.6 3.9 copy-start.1
  366.6 4.5 %copy-start.2 = (bf16[576,6,512]{0,2,1:T(8,128)(2,1)S(1)}, bf16[576,6,512]{0,2,1:T(8,128)(2,1)}, u32[]{:S(2)}) copy-start(bf16[576,6,512]{0,2,1:T(8,128)(2,1)} %copy.13) | copy-start | bytes 10616836
Sparse Core Ops, SparseCore 0:
  9.5 55.4 all-gather.3
  67.2 280.9 all-gather.5
  377.8 49.4 reduce-scatter.1
